TPU v7x, 32 devices: a whole 2x2x4 slice. The times are simulated.
32 devices in a mesh: dist: 4 (over y, x), rows: 8 (over z, core).
Axes of the slice: x: 2, y: 2, z: 4, core: 2. Of those that a mesh axis runs over, the one named last changes fastest.
Arguments:
- volume: bfloat16 [128, 128, 2048], P('rows', None, 'dist'), may hold values from -6 to 6
- kernels: bfloat16 [128, 2, 128, 128], P('rows'), may hold values from -0.09375 to 0.09375
- targets: int32 [128, 2], P('rows'), may hold values from 0 to 7, all different within a row; in each aligned block of 16 rows (0 to 15, 16 to 31, ...) at most 8 rows name the same one
- contrast: bfloat16 [4, 8, 128, 2048], P('dist', 'rows'), may hold values from -6 to 6
- fresnel_numbers: float32 [4], P('dist'), may hold values from 0.4 to 1.6
Outputs:
- gradient: bfloat16 [128, 128, 2048], P('rows', None, 'dist')
Inputs may be any that keep to these rules, and one draw needn't show every extreme that they name: `targets`: each row names 2 different detector blocks; among the rows of one index of rows no detector block is named more than 8 times, and some block is named exactly 8 times.
All inputs are finite; a program needn't handle non-finite values.
Results may differ from a plain program's by a relative error of at most 0.0063.
Values may be sent and summed in bfloat16 or wider, within the bound.
No kernel may reach another device: no remote copies, remote signals or barrier semaphores. Data moves between devices by JAX's collectives and lax.ppermute only.
A program may use at most 128 MiB of HBM per device.

v0:
```python
import functools
import math

import jax
import jax.numpy as jnp
from jax import lax
from jax.experimental import pallas as pl
from jax.experimental.pallas import tpu as pltpu
from jax.sharding import PartitionSpec as P


BF16 = jnp.bfloat16
F32 = jnp.float32
DEEP = 256
LANES = 128
SPLIT = (1,)
TREE = False
MIB = 2**20


def whole(memory_space=pltpu.VMEM):
    return pl.BlockSpec(memory_space=memory_space)


def swap(x, axis, mask):
    size = lax.axis_size(axis)
    return lax.ppermute(x, axis, [(i, i ^ mask) for i in range(size)])


def chunks_of(blk):
    unit = blk // sum(SPLIT)
    starts = [unit * sum(SPLIT[:i]) for i in range(len(SPLIT))]
    return [(start, unit * size) for start, size in zip(starts, SPLIT)]


def cost(flops, nbytes):
    return pl.CostEstimate(flops=flops, bytes_accessed=nbytes, transcendentals=0)


def room(nbytes):
    return pltpu.CompilerParams(vmem_limit_bytes=int(nbytes) + 4 * MIB)


def project_kernel(me_ref, *refs):
    targets_hbm, kernels_hbm, volume_hbm, send_far, send_near, keep_far, keep_near = refs[:7]
    targets, kernels, volume, acc, sems, target_sem = refs[7:]
    vblocks, top, blk, _ = kernels.shape
    near, half = send_near.shape[0], acc.shape[0] // 2
    group = 4
    steps = vblocks // group

    def copies(step):
        part = pl.ds(step * group, group)
        return (
            pltpu.make_async_copy(volume_hbm.at[part], volume.at[part], sems.at[0, step]),
            pltpu.make_async_copy(kernels_hbm.at[part], kernels.at[part], sems.at[1, step]),
        )

    get_targets = pltpu.make_async_copy(targets_hbm, targets, target_sem)
    get_targets.start()
    for step in range(steps):
        for copy in copies(step):
            copy.start()
    acc[...] = jnp.zeros_like(acc)
    get_targets.wait()
    me = me_ref[0]

    def body(step, carry):
        for copy in copies(step):
            copy.wait()
        for i in range(group):
            b = step * group + i
            product = jnp.dot(
                kernels[b].reshape(top * blk, blk), volume[b], preferred_element_type=F32
            )
            product = product.astype(BF16).astype(F32)
            for t in range(top):
                rel = targets[t, b] ^ me
                slot = (rel & 1) * half + (rel >> 1)
                acc[slot] += product[t * blk : (t + 1) * blk]
        return carry

    lax.fori_loop(0, steps, body, 0)
    send_far[...] = acc[half + near :].astype(BF16)
    send_near[...] = acc[half : half + near].astype(BF16)
    keep_far[...] = acc[near:half].astype(BF16)
    keep_near[...] = acc[:near].astype(BF16)


def project(me, targets, kernels, volume, owners):
    vblocks, blk, quarter = volume.shape
    top = kernels.shape[1]
    half = owners // 2
    near = half // 2
    parts = [jax.ShapeDtypeStruct((n, blk, quarter), BF16) for n in (half - near, near)]
    inputs = (targets, kernels, volume)
    return pl.pallas_call(
        project_kernel,
        out_shape=parts + parts,
        in_specs=[whole(pltpu.SMEM)] + [whole(pltpu.HBM)] * 3,
        out_specs=[whole()] * 4,
        scratch_shapes=[
            pltpu.SMEM(targets.shape, jnp.int32),
            pltpu.VMEM(kernels.shape, BF16),
            pltpu.VMEM(volume.shape, BF16),
            pltpu.VMEM((owners, blk, quarter), F32),
            pltpu.SemaphoreType.DMA((2, vblocks)),
            pltpu.SemaphoreType.DMA,
        ],
        compiler_params=room(8 * owners * blk * quarter + 8 * MIB),
        cost_estimate=cost(2 * vblocks * top * blk * blk * quarter, 4 * MIB),
        name="project",
    )(me, *(pltpu.with_memory_space_constraint(x, pltpu.HBM) for x in inputs))


def pair_kernel(keep_ref, came_ref, *out_refs):
    for k, ref in enumerate(out_refs):
        ref[...] = (keep_ref[k].astype(F32) + came_ref[k].astype(F32)).astype(ref.dtype)


def pair_sum(keep, came, dtypes):
    n, blk, quarter = keep.shape
    return pl.pallas_call(
        pair_kernel,
        out_shape=[jax.ShapeDtypeStruct((blk, quarter), dtype) for dtype in dtypes],
        in_specs=[whole()] * 2,
        out_specs=[whole()] * n,
        compiler_params=room(8 * n * blk * quarter),
        cost_estimate=cost(n * blk * quarter, 6 * n * blk * quarter),
        name="pair_sum",
    )(keep, came)


def total_kernel(own_ref, *refs):
    total_ref, rounded_ref = refs[-2:]
    total = own_ref[...]
    for ref in refs[:-2]:
        total += ref[...].astype(F32)
    total_ref[...] = total
    rounded_ref[...] = total.astype(BF16)


def total_sum(own, came):
    return pl.pallas_call(
        total_kernel,
        out_shape=[jax.ShapeDtypeStruct(own.shape, d) for d in (F32, BF16)],
        in_specs=[whole()] * (1 + len(came)),
        out_specs=[whole()] * 2,
        compiler_params=room((10 + 2 * len(came)) * own.size),
        cost_estimate=cost(own.size * len(came), 8 * own.size),
        name="total_sum",
    )(own, *came)


def mm(a, b):
    return jnp.dot(a, b, precision=lax.Precision.HIGHEST, preferred_element_type=F32)


def turns(shape, period):
    a = lax.broadcasted_iota(jnp.int32, shape, 0)
    b = lax.broadcasted_iota(jnp.int32, shape, 1)
    angle = (a * b % period).astype(F32) * (2.0 * math.pi / period)
    return jnp.cos(angle), jnp.sin(angle)


def frequencies(short, long):
    k1 = lax.broadcasted_iota(jnp.int32, (short, long), 0)
    k2 = lax.broadcasted_iota(jnp.int32, (short, long), 1)
    freq = k1 + short * k2
    return jnp.minimum(freq, short * long - freq).astype(F32)


def circulant(spec):
    short, long = spec.shape
    width = short * long
    long_c, long_s = turns((long, long), long)
    twist_c, twist_s = turns((short, long), width)
    short_c, short_s = turns((short, short), short)
    yc, ys = mm(spec, long_c), mm(spec, long_s)
    re = yc * twist_c - ys * twist_s
    im = yc * twist_s + ys * twist_c
    g = (mm(short_c, re) - mm(short_s, im)) * (1.0 / width)
    line = jnp.concatenate([g[i : i + 1] for i in range(short)], axis=1)
    spread = jnp.broadcast_to(line, (LANES, width))
    return pltpu.roll(spread, 0, 1, stride=1, stride_axis=0).astype(BF16)


def store_table(table_ref, matrix):
    width, total = matrix.shape[1], table_ref.shape[1]
    for top in range(0, DEEP, LANES):
        rows = slice(top, top + LANES)
        if top:
            table_ref[rows, :top] = matrix[:, width - top :]
        for start in range(top, total, width):
            size = min(width, total - start)
            table_ref[rows, start : start + size] = matrix[:, :size]


def contrast_factor(number, width):
    short, long = width // LANES, LANES
    freq = frequencies(short, long)
    return 2.0 * jnp.sin(jnp.pi * jnp.full((short, long), number, F32) * freq * freq / width)


def circ_kernel(number_ref, spread_ref, table_ref):
    width = table_ref.shape[1] // 2
    spread_ref[...] = jnp.full(spread_ref.shape, number_ref[0], F32)
    store_table(table_ref, circulant(contrast_factor(number_ref[0], width)))


def circ(number, width):
    return pl.pallas_call(
        circ_kernel,
        out_shape=(
            jax.ShapeDtypeStruct((8, LANES), F32),
            jax.ShapeDtypeStruct((DEEP, 2 * width), BF16),
        ),
        in_specs=[whole(pltpu.SMEM)],
        out_specs=[whole()] * 2,
        compiler_params=room(8 * MIB),
        cost_estimate=cost(2**24, 3 * MIB),
        name="circ",
    )(number)


def term_kernel(number_ref, me_ref, contrast_ref, table_ref, *out_refs):
    n_dist = len(out_refs)
    blk, width = contrast_ref.shape
    quarter = width // n_dist
    me = me_ref[0]
    value = jnp.broadcast_to(number_ref[:1, :1], (16, quarter))
    for k, ref in enumerate(out_refs):
        at = (me ^ k) * quarter
        total = jnp.zeros((blk, quarter), F32)
        for i in range(width // DEEP):
            start = pl.multiple_of(lax.rem(width - i * DEEP + at, width), 128)
            total += jnp.dot(
                contrast_ref[:, i * DEEP : (i + 1) * DEEP],
                table_ref[:, pl.ds(start, quarter)],
                preferred_element_type=F32,
            )
        ref[:blk] = total.astype(BF16)
        if k:
            rest, parts = value, []
            for _ in range(3):
                parts.append(rest.astype(BF16).astype(F32))
                rest = rest - parts[-1]
            which = lax.broadcasted_iota(jnp.int32, value.shape, 0)
            packed = jnp.where(which == 0, parts[0], jnp.where(which == 1, parts[1], parts[2]))
            ref[blk:] = packed.astype(BF16)


def terms_of(number, me, contrast, table, n_dist):
    blk, width = contrast.shape
    quarter = width // n_dist
    return pl.pallas_call(
        term_kernel,
        out_shape=[
            jax.ShapeDtypeStruct((blk + (16 if k else 0), quarter), BF16) for k in range(n_dist)
        ],
        in_specs=[whole(), whole(pltpu.SMEM), whole(), whole()],
        out_specs=[whole()] * n_dist,
        compiler_params=room(12 * MIB),
        cost_estimate=cost(2 * blk * width * width, 3 * MIB),
        name="terms",
    )(number, me, contrast, table)


def table_kernel(number_ref, *refs):
    term_refs, (table_ref, sum_ref) = refs[:-2], refs[-2:]
    blk, quarter = sum_ref.shape
    width = table_ref.shape[1] - quarter
    short, long = width // LANES, LANES
    freq = frequencies(short, long)
    total = term_refs[0][...].astype(F32)
    number = jnp.broadcast_to(number_ref[:1], (short, long))
    factor = jnp.sin(jnp.pi * number * freq * freq / width)
    squares = factor * factor
    for ref in term_refs[1:]:
        total += ref[:blk].astype(F32)
        parts = ref[blk:, :long].astype(F32)
        number = (parts[0:1] + parts[1:2]) + parts[2:3]
        factor = jnp.sin(jnp.pi * jnp.broadcast_to(number, (short, long)) * freq * freq / width)
        squares += factor * factor
    sum_ref[...] = total
    matrix = circulant(4.0 * squares - 2.0 * len(term_refs))
    store_table(table_ref, matrix)


def table_of(number, terms):
    n_dist = len(terms)
    blk, quarter = terms[0].shape
    width = n_dist * quarter
    return pl.pallas_call(
        table_kernel,
        out_shape=(
            jax.ShapeDtypeStruct((DEEP, width + quarter), BF16),
            jax.ShapeDtypeStruct((blk, quarter), F32),
        ),
        in_specs=[whole()] * (1 + n_dist),
        out_specs=[whole()] * 2,
        compiler_params=room(12 * MIB),
        cost_estimate=cost(2**24, 3 * MIB),
        name="table",
    )(number, *terms)


def filter_kernel(n_dist, me_ref, own_ref, term_ref, table_ref, *refs):
    parts, out_refs = refs[:n_dist], refs[n_dist:]
    blk, quarter = own_ref.shape
    width = n_dist * quarter
    me = me_ref[0]
    total = (2.0 * n_dist) * own_ref[...] + term_ref[...]
    for k, ref in enumerate(parts):
        for h in range(quarter // DEEP):
            start = (me - (me ^ k)) * quarter - h * DEEP + width
            start = pl.multiple_of(lax.rem(start, width), LANES)
            total += jnp.dot(
                ref[:, h * DEEP : (h + 1) * DEEP],
                table_ref[:, pl.ds(start, quarter)],
                preferred_element_type=F32,
            )
    for ref, (start, rows) in zip(out_refs, chunks_of(blk)):
        ref[...] = total[start : start + rows].astype(BF16)


def filtered(me, own, term, table, parts):
    blk, quarter = own.shape
    n_dist = len(parts)
    outs = [jax.ShapeDtypeStruct((rows, quarter), BF16) for _, rows in chunks_of(blk)]
    return pl.pallas_call(
        functools.partial(filter_kernel, n_dist),
        out_shape=outs,
        in_specs=[whole(pltpu.SMEM)] + [whole()] * (3 + n_dist),
        out_specs=[whole()] * len(outs),
        compiler_params=room(4 * MIB),
        cost_estimate=cost(2 * blk * quarter * quarter * n_dist, 3 * MIB),
        name="filter",
    )(me, own, term, table, *parts)


def back_kernel(owners, me_ref, targets_ref, kernels_ref, *refs):
    parts, (out_hbm, chosen, out, sems) = refs[:-4], refs[-4:]
    vblocks, blk, _ = out.shape
    top = kernels_ref.shape[1]
    for c, (start, rows) in enumerate(chunks_of(blk)):
        for k in range(owners):
            chosen[k, start : start + rows] = parts[c * owners + k][...]
    me = me_ref[0]
    group = 4
    copies = []
    for step in range(vblocks // group):
        for b in range(step * group, (step + 1) * group):
            picked = [chosen[targets_ref[t, b] ^ me] for t in range(top)]
            out[b] = lax.dot_general(
                kernels_ref[b].reshape(top * blk, blk),
                jnp.concatenate(picked, axis=0),
                (((0,), (0,)), ((), ())),
                preferred_element_type=F32,
            ).astype(BF16)
        part = pl.ds(step * group, group)
        copies.append(pltpu.make_async_copy(out.at[part], out_hbm.at[part], sems.at[step]))
        copies[-1].start()
    for copy in copies:
        copy.wait()


def back(me, targets, kernels, parts, owners):
    vblocks, top, blk, _ = kernels.shape
    quarter = parts[0].shape[1]
    return pl.pallas_call(
        functools.partial(back_kernel, owners),
        out_shape=jax.ShapeDtypeStruct((vblocks, blk, quarter), BF16),
        in_specs=[whole(pltpu.SMEM)] * 2 + [whole()] * (1 + len(parts)),
        out_specs=whole(pltpu.HBM),
        scratch_shapes=[
            pltpu.VMEM((owners, blk, quarter), BF16),
            pltpu.VMEM((vblocks, blk, quarter), BF16),
            pltpu.SemaphoreType.DMA((vblocks,)),
        ],
        compiler_params=room(2 * (owners + vblocks) * blk * quarter + 6 * MIB),
        cost_estimate=cost(2 * vblocks * top * blk * blk * quarter, 4 * MIB),
        name="back",
    )(me, targets, kernels, *parts)


def source(rel):
    low = 1 if rel & 1 else (rel & -rel if TREE else rel)
    return rel ^ low, low


def shards(volume, kernels, targets, contrast, fresnel_numbers):
    owners, n_dist = lax.axis_size("rows"), lax.axis_size("dist")
    me_rows = lax.axis_index("rows").astype(jnp.int32).reshape(1)
    me_dist = lax.axis_index("dist").astype(jnp.int32).reshape(1)
    half = owners // 2
    near = half // 2
    targets = targets.T

    send_far, send_near, keep_far, keep_near = project(me_rows, targets, kernels, volume, owners)
    number, contrast_table = circ(fresnel_numbers, contrast.shape[-1])
    came_far = swap(send_far, "rows", 1)
    came_near = swap(send_near, "rows", 1)
    far_sums = pair_sum(keep_far, came_far, [BF16] * (half - near))
    own, *near_sums = pair_sum(keep_near, came_near, [F32] + [BF16] * (near - 1))
    arrived = []
    for k, x in enumerate([*near_sums, *far_sums]):
        arrived.append(swap(x, "rows", 2 * (k + 1)))

    terms = terms_of(number, me_dist, contrast[0, 0], contrast_table, n_dist)
    came = [terms[0]]
    for k in range(1, n_dist):
        came.append(swap(terms[k], "dist", k))
    table, term = table_of(number, came)

    total, rounded = total_sum(own, arrived)
    parts = [rounded]
    for k in range(1, n_dist):
        parts.append(swap(rounded, "dist", k))
    images = filtered(me_dist, total, term, table, parts)
    pieces = []
    for image in images:
        found = [image]
        for rel in range(1, owners):
            origin, mask = source(rel)
            found.append(swap(found[origin], "rows", mask))
        pieces += found
    return back(me_rows, targets, kernels, pieces, owners)


def solution(mesh):
    in_specs = (
        P("rows", None, "dist"),
        P("rows", None, None, None),
        P("rows", None),
        P("dist", "rows", None, None),
        P("dist"),
    )
    out_specs = P("rows", None, "dist")

    return jax.shard_map(shards, mesh=mesh, in_specs=in_specs, out_specs=out_specs, check_vma=False)
```

profile of v0, /device:TPU:0, one launch (start us, length us, event | category | flops | bytes accessed | tf_op | source)
XLA Modules:
  0.0 51.4 jit_solution(14997338341103566559)
XLA Ops:
  0.0 0.0 copy-start.2
  0.0 3.3 %project.1 = (bf16[2,128,512]{2,1,0:T(8,128)(2,1)S(1)}, bf16[2,128,512]{2,1,0:T(8,128)(2,1)S(1)}, bf16[2,128,512]{2,1,0:T(8,128)(2,1)S(1)}, bf16[2,128,512]{2,1,0:T(8,128)(2,1)S(1)}) custom-call(s32[1]{0:T(128)} %bitcast.me_ref, s32[2,16]{1,0:T(2,128)} %bitcast.4, bf16[16,2,128,128]{3,2,1,0:T(8,128)(2,1)} %kernels_ref.1, bf16[16,128,512]{2,1,0:T(8,128)(2,1)} %refs_2_.1), custom_call_target="tpu_custom_call" | custom-call | flops 536870912 | bytes 4194304 | tf_op jit(solution)/shard_map/project/pallas_call | solution.py:97
  3.3 0.6 %collective-permute-start = (bf16[2,128,512]{2,1,0:T(8,128)(2,1)S(1)}, bf16[2,128,512]{2,1,0:T(8,128)(2,1)S(1)}, u32[]{:S(2)}, u32[]{:S(2)}) collective-permute-start(bf16[2,128,512]{2,1,0:T(8,128)(2,1)S(1)} %get-tuple-element.24), channel_id=1, source_target_pairs={{0,1},{1,0},{2,3},{3,2},{4,5},{5,4},{6,7},{7,6},{8,9},{9,8},{10,11... | collective-permute-start | bytes 786440 | tf_op jit(solution)/shard_map/ppermute | solution.py:27
  3.8 0.1 collective-permute-start.2
  4.6 0.9 %circ.1 = (f32[8,128]{1,0:T(8,128)S(1)}, bf16[256,4096]{1,0:T(8,128)(2,1)S(1)}) custom-call(f32[1]{0:T(128)S(6)} %copy.6.number_ref), custom_call_target="tpu_custom_call" | custom-call | flops 16777216 | bytes 3145728 | tf_op jit(solution)/shard_map/circ/pallas_call | solution.py:212
  5.5 0.0 collective-permute-done.came_ref
  5.5 0.1 pair_sum.2
  5.6 3.1 %collective-permute-start.1 = (bf16[128,512]{1,0:T(8,128)(2,1)S(1)}, bf16[128,512]{1,0:T(8,128)(2,1)S(1)}, u32[]{:S(2)}, u32[]{:S(2)}) collective-permute-start(bf16[128,512]{1,0:T(8,128)(2,1)S(1)} %get-tuple-element.26), channel_id=1, source_target_pairs={{0,2},{1,3},{2,0},{3,1},{4,6},{5,7},{6,4},{7,5},{8,10},{9,11},{10,... | collective-permute-start | bytes 393224 | tf_op jit(solution)/shard_map/ppermute | solution.py:27
  8.6 0.0 copy-done.2
  8.6 1.3 %terms.1 = (bf16[128,512]{1,0:T(8,128)(2,1)S(1)}, bf16[144,512]{1,0:T(8,128)(2,1)S(1)}, bf16[144,512]{1,0:T(8,128)(2,1)S(1)}, bf16[144,512]{1,0:T(8,128)(2,1)S(1)}) custom-call(f32[8,128]{1,0:T(8,128)S(1)} %get-tuple-element.32.number_ref, s32[1]{0:T(128)} %bitcast.2.me_ref, bf16[128,2048]{1,0:T(8,128)(2,1)S(1)} %bitcast.6, ...), custom_call_target="tpu_custom_call" | custom-call | flops 1073741824 | bytes 3145728 | tf_op jit(solution)/shard_map/terms/pallas_call | solution.py:256
  9.9 1.5 %collective-permute-start.5 = (bf16[144,512]{1,0:T(8,128)(2,1)S(1)}, bf16[144,512]{1,0:T(8,128)(2,1)S(1)}, u32[]{:S(2)}, u32[]{:S(2)}) collective-permute-start(bf16[144,512]{1,0:T(8,128)(2,1)S(1)} %get-tuple-element.35), channel_id=1, source_target_pairs={{0,8},{8,0},{16,24},{24,16},{1,9},{9,1},{17,25},{25,17},{2,10},{10... | collective-permute-start | bytes 442376 | tf_op jit(solution)/shard_map/ppermute | solution.py:27
  11.5 0.0 collective-permute-done.2.came_ref
  11.5 0.0 copy-start
  11.5 0.0 copy-start.1
  11.5 0.1 pair_sum.3
  11.6 2.7 %collective-permute-start.3 = (bf16[128,512]{1,0:T(8,128)(2,1)S(1)}, bf16[128,512]{1,0:T(8,128)(2,1)S(1)}, u32[]{:S(2)}, u32[]{:S(2)}) collective-permute-start(bf16[128,512]{1,0:T(8,128)(2,1)S(1)} %get-tuple-element.29), channel_id=1, source_target_pairs={{0,4},{1,5},{2,6},{3,7},{4,0},{5,1},{6,2},{7,3},{8,12},{9,13},{10,... | collective-permute-start | bytes 393224 | tf_op jit(solution)/shard_map/ppermute | solution.py:27
  14.2 0.2 collective-permute-start.4
  14.4 1.5 %collective-permute-start.6 = (bf16[144,512]{1,0:T(8,128)(2,1)S(1)}, bf16[144,512]{1,0:T(8,128)(2,1)S(1)}, u32[]{:S(2)}, u32[]{:S(2)}) collective-permute-start(bf16[144,512]{1,0:T(8,128)(2,1)S(1)} %get-tuple-element.36), channel_id=1, source_target_pairs={{0,16},{8,24},{16,0},{24,8},{1,17},{9,25},{17,1},{25,9},{2,18},{10... | collective-permute-start | bytes 442376 | tf_op jit(solution)/shard_map/ppermute | solution.py:27
  15.9 0.0 collective-permute-done.1.refs_0_
  16.0 0.3 collective-permute-start.7
  16.2 6.8 %collective-permute-done.3.refs_1_ = bf16[128,512]{1,0:T(8,128)(2,1)S(1)} collective-permute-done((bf16[128,512]{1,0:T(8,128)(2,1)S(1)}, bf16[128,512]{1,0:T(8,128)(2,1)S(1)}, u32[]{:S(2)}, u32[]{:S(2)}) %collective-permute-start.3) | collective-permute-done | bytes 131104 | tf_op jit(solution)/shard_map/ppermute | solution.py:27
  23.1 0.0 collective-permute-done.4.refs_2_
  23.1 0.1 total_sum.1
  23.1 1.3 %collective-permute-start.8 = (bf16[128,512]{1,0:T(8,128)(2,1)S(1)}, bf16[128,512]{1,0:T(8,128)(2,1)S(1)}, u32[]{:S(2)}, u32[]{:S(2)}) collective-permute-start(bf16[128,512]{1,0:T(8,128)(2,1)S(1)} %get-tuple-element.40.refs_0_), channel_id=1, source_target_pairs={{0,8},{8,0},{16,24},{24,16},{1,9},{9,1},{17,25},{25,17},{2,10},{10... | collective-permute-start | bytes 393224 | tf_op jit(solution)/shard_map/ppermute | solution.py:27
  24.5 1.5 %collective-permute-start.9 = (bf16[128,512]{1,0:T(8,128)(2,1)S(1)}, bf16[128,512]{1,0:T(8,128)(2,1)S(1)}, u32[]{:S(2)}, u32[]{:S(2)}) collective-permute-start(bf16[128,512]{1,0:T(8,128)(2,1)S(1)} %get-tuple-element.40.refs_0_), channel_id=1, source_target_pairs={{0,16},{8,24},{16,0},{24,8},{1,17},{9,25},{17,1},{25,9},{2,18},{10... | collective-permute-start | bytes 393224 | tf_op jit(solution)/shard_map/ppermute | solution.py:27
  26.0 0.0 collective-permute-done.5.refs_1_
  26.0 0.7 %collective-permute-start.10 = (bf16[128,512]{1,0:T(8,128)(2,1)S(1)}, bf16[128,512]{1,0:T(8,128)(2,1)S(1)}, u32[]{:S(2)}, u32[]{:S(2)}) collective-permute-start(bf16[128,512]{1,0:T(8,128)(2,1)S(1)} %get-tuple-element.40.refs_0_), channel_id=1, source_target_pairs={{0,24},{8,16},{16,8},{24,0},{1,25},{9,17},{17,9},{25,1},{2,26},{10... | collective-permute-start | bytes 393224 | tf_op jit(solution)/shard_map/ppermute | solution.py:27
  26.7 0.0 collective-permute-done.6.refs_2_
  26.7 0.0 collective-permute-done.7.refs_3_
  26.7 1.0 %table.1 = (bf16[256,2560]{1,0:T(8,128)(2,1)S(1)}, f32[128,512]{1,0:T(8,128)S(1)}) custom-call(f32[8,128]{1,0:T(8,128)S(1)} %get-tuple-element.32.number_ref, bf16[128,512]{1,0:T(8,128)(2,1)S(1)} %get-tuple-element.34.refs_0_, bf16[144,512]{1,0:T(8,128)(2,1)S(1)} %collective-permute-done.5.refs_1_, bf16[144,512]{1,0:T(8,128)(2,1)S(1)} %collective-permute-done.6.refs_2_, ...), custom_call_target="tpu_custom_call" | custom-call | flops 16777216 | bytes 3145728 | tf_op jit(solution)/shard_map/table/pallas_call | solution.py:294
  27.8 1.8 %collective-permute-done.8.refs_1_ = bf16[128,512]{1,0:T(8,128)(2,1)S(1)} collective-permute-done((bf16[128,512]{1,0:T(8,128)(2,1)S(1)}, bf16[128,512]{1,0:T(8,128)(2,1)S(1)}, u32[]{:S(2)}, u32[]{:S(2)}) %collective-permute-start.8) | collective-permute-done | bytes 131104 | tf_op jit(solution)/shard_map/ppermute | solution.py:27
  29.6 1.4 %collective-permute-done.9.refs_2_ = bf16[128,512]{1,0:T(8,128)(2,1)S(1)} collective-permute-done((bf16[128,512]{1,0:T(8,128)(2,1)S(1)}, bf16[128,512]{1,0:T(8,128)(2,1)S(1)}, u32[]{:S(2)}, u32[]{:S(2)}) %collective-permute-start.9) | collective-permute-done | bytes 131104 | tf_op jit(solution)/shard_map/ppermute | solution.py:27
  31.0 1.3 %collective-permute-done.10.refs_3_ = bf16[128,512]{1,0:T(8,128)(2,1)S(1)} collective-permute-done((bf16[128,512]{1,0:T(8,128)(2,1)S(1)}, bf16[128,512]{1,0:T(8,128)(2,1)S(1)}, u32[]{:S(2)}, u32[]{:S(2)}) %collective-permute-start.10) | collective-permute-done | bytes 131104 | tf_op jit(solution)/shard_map/ppermute | solution.py:27
  32.3 0.4 filter.1.refs_0_
  32.7 3.4 %collective-permute-start.12 = (bf16[128,512]{1,0:T(8,128)(2,1)S(1)}, bf16[128,512]{1,0:T(8,128)(2,1)S(1)}, u32[]{:S(2)}, u32[]{:S(2)}) collective-permute-start(bf16[128,512]{1,0:T(8,128)(2,1)S(1)} %filter.1.refs_0_), channel_id=1, source_target_pairs={{0,2},{1,3},{2,0},{3,1},{4,6},{5,7},{6,4},{7,5},{8,10},{9,11},{10,... | collective-permute-start | bytes 393224 | tf_op jit(solution)/shard_map/ppermute | solution.py:27
  36.2 0.2 collective-permute-start.14
  36.4 2.2 %collective-permute-start.16 = (bf16[128,512]{1,0:T(8,128)(2,1)S(1)}, bf16[128,512]{1,0:T(8,128)(2,1)S(1)}, u32[]{:S(2)}, u32[]{:S(2)}) collective-permute-start(bf16[128,512]{1,0:T(8,128)(2,1)S(1)} %filter.1.refs_0_), channel_id=1, source_target_pairs={{0,6},{1,7},{2,4},{3,5},{4,2},{5,3},{6,0},{7,1},{8,14},{9,15},{10,... | collective-permute-start | bytes 393224 | tf_op jit(solution)/shard_map/ppermute | solution.py:27
  38.6 0.0 collective-permute-start.11
  38.6 1.4 %collective-permute-done.12.refs_2_ = bf16[128,512]{1,0:T(8,128)(2,1)S(1)} collective-permute-done((bf16[128,512]{1,0:T(8,128)(2,1)S(1)}, bf16[128,512]{1,0:T(8,128)(2,1)S(1)}, u32[]{:S(2)}, u32[]{:S(2)}) %collective-permute-start.12) | collective-permute-done | bytes 131104 | tf_op jit(solution)/shard_map/ppermute | solution.py:27
  40.1 0.0 collective-permute-start.13
  40.1 7.4 %collective-permute-done.14.refs_4_ = bf16[128,512]{1,0:T(8,128)(2,1)S(1)} collective-permute-done((bf16[128,512]{1,0:T(8,128)(2,1)S(1)}, bf16[128,512]{1,0:T(8,128)(2,1)S(1)}, u32[]{:S(2)}, u32[]{:S(2)}) %collective-permute-start.14) | collective-permute-done | bytes 131104 | tf_op jit(solution)/shard_map/ppermute | solution.py:27
  47.4 0.0 collective-permute-start.15
  47.4 0.0 collective-permute-done.16.refs_6_
  47.4 0.5 collective-permute-start.17
  47.9 0.0 collective-permute-done.11.refs_1_
  48.0 0.0 collective-permute-done.13.refs_3_
  48.0 0.8 %collective-permute-done.15.refs_5_ = bf16[128,512]{1,0:T(8,128)(2,1)S(1)} collective-permute-done((bf16[128,512]{1,0:T(8,128)(2,1)S(1)}, bf16[128,512]{1,0:T(8,128)(2,1)S(1)}, u32[]{:S(2)}, u32[]{:S(2)}) %collective-permute-start.15) | collective-permute-done | bytes 131104 | tf_op jit(solution)/shard_map/ppermute | solution.py:27
  48.8 0.2 collective-permute-done.17.refs_7_
  49.0 0.0 copy-done
  49.0 0.0 copy-done.1
  49.0 2.4 %back.1 = bf16[16,128,512]{2,1,0:T(8,128)(2,1)} custom-call(s32[1]{0:T(128)} %bitcast.me_ref, s32[2,16]{1,0:T(2,128)S(1)} %bitcast.5, bf16[16,2,128,128]{3,2,1,0:T(8,128)(2,1)S(1)} %copy-done, bf16[128,512]{1,0:T(8,128)(2,1)S(1)} %filter.1.refs_0_, bf16[128,512]{1,0:T(8,128)(2,1)S(1)} %collective-permute-done.11.refs_1_, ...), custom_call_target="tpu_custom_call" | custom-call | flops 536870912 | bytes 4194304 | tf_op jit(solution)/shard_map/back/pallas_call | solution.py:371
Async XLA Ops:
  0.0 8.6 %copy-start.2 = (bf16[1,1,128,2048]{3,2,1,0:T(8,128)(2,1)S(1)}, bf16[1,1,128,2048]{3,2,1,0:T(8,128)(2,1)}, u32[]{:S(2)}) copy-start(bf16[1,1,128,2048]{3,2,1,0:T(8,128)(2,1)} %param.8) | copy-start | bytes 1572868
  3.3 2.2 %collective-permute-start = (bf16[2,128,512]{2,1,0:T(8,128)(2,1)S(1)}, bf16[2,128,512]{2,1,0:T(8,128)(2,1)S(1)}, u32[]{:S(2)}, u32[]{:S(2)}) collective-permute-start(bf16[2,128,512]{2,1,0:T(8,128)(2,1)S(1)} %get-tuple-element.24), channel_id=1, source_target_pairs={{0,1},{1,0},{2,3},{3,2},{4,5},{5,4},{6,7},{7,6},{8,9},{9,8},{10,11... | collective-permute-start | bytes 786440 | tf_op jit(solution)/shard_map/ppermute | solution.py:27
  3.8 7.6 %collective-permute-start.2 = (bf16[2,128,512]{2,1,0:T(8,128)(2,1)S(1)}, bf16[2,128,512]{2,1,0:T(8,128)(2,1)S(1)}, u32[]{:S(2)}, u32[]{:S(2)}) collective-permute-start(bf16[2,128,512]{2,1,0:T(8,128)(2,1)S(1)} %get-tuple-element.28), channel_id=1, source_target_pairs={{0,1},{1,0},{2,3},{3,2},{4,5},{5,4},{6,7},{7,6},{8,9},{9,8},{10,11... | collective-permute-start | bytes 786440 | tf_op jit(solution)/shard_map/ppermute | solution.py:27
  5.6 10.4 %collective-permute-start.1 = (bf16[128,512]{1,0:T(8,128)(2,1)S(1)}, bf16[128,512]{1,0:T(8,128)(2,1)S(1)}, u32[]{:S(2)}, u32[]{:S(2)}) collective-permute-start(bf16[128,512]{1,0:T(8,128)(2,1)S(1)} %get-tuple-element.26), channel_id=1, source_target_pairs={{0,2},{1,3},{2,0},{3,1},{4,6},{5,7},{6,4},{7,5},{8,10},{9,11},{10,... | collective-permute-start | bytes 393224 | tf_op jit(solution)/shard_map/ppermute | solution.py:27
  9.9 16.0 %collective-permute-start.5 = (bf16[144,512]{1,0:T(8,128)(2,1)S(1)}, bf16[144,512]{1,0:T(8,128)(2,1)S(1)}, u32[]{:S(2)}, u32[]{:S(2)}) collective-permute-start(bf16[144,512]{1,0:T(8,128)(2,1)S(1)} %get-tuple-element.35), channel_id=1, source_target_pairs={{0,8},{8,0},{16,24},{24,16},{1,9},{9,1},{17,25},{25,17},{2,10},{10... | collective-permute-start | bytes 442376 | tf_op jit(solution)/shard_map/ppermute | solution.py:27
  11.5 37.5 %copy-start = (bf16[16,2,128,128]{3,2,1,0:T(8,128)(2,1)S(1)}, bf16[16,2,128,128]{3,2,1,0:T(8,128)(2,1)}, u32[]{:S(2)}) copy-start(bf16[16,2,128,128]{3,2,1,0:T(8,128)(2,1)} %kernels_ref.1) | copy-start | bytes 3145732
  11.5 37.5 %copy-start.1 = (s32[16,2]{0,1:T(2,128)S(1)}, s32[16,2]{0,1:T(2,128)}, u32[]{:S(2)}) copy-start(s32[16,2]{0,1:T(2,128)} %param.7) | copy-start | bytes 388
  11.6 11.5 %collective-permute-start.3 = (bf16[128,512]{1,0:T(8,128)(2,1)S(1)}, bf16[128,512]{1,0:T(8,128)(2,1)S(1)}, u32[]{:S(2)}, u32[]{:S(2)}) collective-permute-start(bf16[128,512]{1,0:T(8,128)(2,1)S(1)} %get-tuple-element.29), channel_id=1, source_target_pairs={{0,4},{1,5},{2,6},{3,7},{4,0},{5,1},{6,2},{7,3},{8,12},{9,13},{10,... | collective-permute-start | bytes 393224 | tf_op jit(solution)/shard_map/ppermute | solution.py:27
  14.2 8.9 %collective-permute-start.4 = (bf16[128,512]{1,0:T(8,128)(2,1)S(1)}, bf16[128,512]{1,0:T(8,128)(2,1)S(1)}, u32[]{:S(2)}, u32[]{:S(2)}) collective-permute-start(bf16[128,512]{1,0:T(8,128)(2,1)S(1)} %get-tuple-element.30), channel_id=1, source_target_pairs={{0,6},{1,7},{2,4},{3,5},{4,2},{5,3},{6,0},{7,1},{8,14},{9,15},{10,... | collective-permute-start | bytes 393224 | tf_op jit(solution)/shard_map/ppermute | solution.py:27
  14.4 12.3 %collective-permute-start.6 = (bf16[144,512]{1,0:T(8,128)(2,1)S(1)}, bf16[144,512]{1,0:T(8,128)(2,1)S(1)}, u32[]{:S(2)}, u32[]{:S(2)}) collective-permute-start(bf16[144,512]{1,0:T(8,128)(2,1)S(1)} %get-tuple-element.36), channel_id=1, source_target_pairs={{0,16},{8,24},{16,0},{24,8},{1,17},{9,25},{17,1},{25,9},{2,18},{10... | collective-permute-start | bytes 442376 | tf_op jit(solution)/shard_map/ppermute | solution.py:27
  16.0 10.8 %collective-permute-start.7 = (bf16[144,512]{1,0:T(8,128)(2,1)S(1)}, bf16[144,512]{1,0:T(8,128)(2,1)S(1)}, u32[]{:S(2)}, u32[]{:S(2)}) collective-permute-start(bf16[144,512]{1,0:T(8,128)(2,1)S(1)} %get-tuple-element.37), channel_id=1, source_target_pairs={{0,24},{8,16},{16,8},{24,0},{1,25},{9,17},{17,9},{25,1},{2,26},{10... | collective-permute-start | bytes 442376 | tf_op jit(solution)/shard_map/ppermute | solution.py:27
  23.1 6.4 %collective-permute-start.8 = (bf16[128,512]{1,0:T(8,128)(2,1)S(1)}, bf16[128,512]{1,0:T(8,128)(2,1)S(1)}, u32[]{:S(2)}, u32[]{:S(2)}) collective-permute-start(bf16[128,512]{1,0:T(8,128)(2,1)S(1)} %get-tuple-element.40.refs_0_), channel_id=1, source_target_pairs={{0,8},{8,0},{16,24},{24,16},{1,9},{9,1},{17,25},{25,17},{2,10},{10... | collective-permute-start | bytes 393224 | tf_op jit(solution)/shard_map/ppermute | solution.py:27
  24.5 6.6 %collective-permute-start.9 = (bf16[128,512]{1,0:T(8,128)(2,1)S(1)}, bf16[128,512]{1,0:T(8,128)(2,1)S(1)}, u32[]{:S(2)}, u32[]{:S(2)}) collective-permute-start(bf16[128,512]{1,0:T(8,128)(2,1)S(1)} %get-tuple-element.40.refs_0_), channel_id=1, source_target_pairs={{0,16},{8,24},{16,0},{24,8},{1,17},{9,25},{17,1},{25,9},{2,18},{10... | collective-permute-start | bytes 393224 | tf_op jit(solution)/shard_map/ppermute | solution.py:27
  26.0 6.3 %collective-permute-start.10 = (bf16[128,512]{1,0:T(8,128)(2,1)S(1)}, bf16[128,512]{1,0:T(8,128)(2,1)S(1)}, u32[]{:S(2)}, u32[]{:S(2)}) collective-permute-start(bf16[128,512]{1,0:T(8,128)(2,1)S(1)} %get-tuple-element.40.refs_0_), channel_id=1, source_target_pairs={{0,24},{8,16},{16,8},{24,0},{1,25},{9,17},{17,9},{25,1},{2,26},{10... | collective-permute-start | bytes 393224 | tf_op jit(solution)/shard_map/ppermute | solution.py:27
  32.7 7.3 %collective-permute-start.12 = (bf16[128,512]{1,0:T(8,128)(2,1)S(1)}, bf16[128,512]{1,0:T(8,128)(2,1)S(1)}, u32[]{:S(2)}, u32[]{:S(2)}) collective-permute-start(bf16[128,512]{1,0:T(8,128)(2,1)S(1)} %filter.1.refs_0_), channel_id=1, source_target_pairs={{0,2},{1,3},{2,0},{3,1},{4,6},{5,7},{6,4},{7,5},{8,10},{9,11},{10,... | collective-permute-start | bytes 393224 | tf_op jit(solution)/shard_map/ppermute | solution.py:27
  36.2 11.3 %collective-permute-start.14 = (bf16[128,512]{1,0:T(8,128)(2,1)S(1)}, bf16[128,512]{1,0:T(8,128)(2,1)S(1)}, u32[]{:S(2)}, u32[]{:S(2)}) collective-permute-start(bf16[128,512]{1,0:T(8,128)(2,1)S(1)} %filter.1.refs_0_), channel_id=1, source_target_pairs={{0,4},{1,5},{2,6},{3,7},{4,0},{5,1},{6,2},{7,3},{8,12},{9,13},{10,... | collective-permute-start | bytes 393224 | tf_op jit(solution)/shard_map/ppermute | solution.py:27
  36.4 11.1 %collective-permute-start.16 = (bf16[128,512]{1,0:T(8,128)(2,1)S(1)}, bf16[128,512]{1,0:T(8,128)(2,1)S(1)}, u32[]{:S(2)}, u32[]{:S(2)}) collective-permute-start(bf16[128,512]{1,0:T(8,128)(2,1)S(1)} %filter.1.refs_0_), channel_id=1, source_target_pairs={{0,6},{1,7},{2,4},{3,5},{4,2},{5,3},{6,0},{7,1},{8,14},{9,15},{10,... | collective-permute-start | bytes 393224 | tf_op jit(solution)/shard_map/ppermute | solution.py:27
  38.6 9.3 %collective-permute-start.11 = (bf16[128,512]{1,0:T(8,128)(2,1)S(1)}, bf16[128,512]{1,0:T(8,128)(2,1)S(1)}, u32[]{:S(2)}, u32[]{:S(2)}) collective-permute-start(bf16[128,512]{1,0:T(8,128)(2,1)S(1)} %filter.1.refs_0_), channel_id=1, source_target_pairs={{0,1},{1,0},{2,3},{3,2},{4,5},{5,4},{6,7},{7,6},{8,9},{9,8},{10,11... | collective-permute-start | bytes 393224 | tf_op jit(solution)/shard_map/ppermute | solution.py:27
  40.1 7.9 %collective-permute-start.13 = (bf16[128,512]{1,0:T(8,128)(2,1)S(1)}, bf16[128,512]{1,0:T(8,128)(2,1)S(1)}, u32[]{:S(2)}, u32[]{:S(2)}) collective-permute-start(bf16[128,512]{1,0:T(8,128)(2,1)S(1)} %collective-permute-done.12.refs_2_), channel_id=1, source_target_pairs={{0,1},{1,0},{2,3},{3,2},{4,5},{5,4},{6,7},{7,6},{8,9},{9,8},{10,11... | collective-permute-start | bytes 393224 | tf_op jit(solution)/shard_map/ppermute | solution.py:27
  47.4 1.3 %collective-permute-start.15 = (bf16[128,512]{1,0:T(8,128)(2,1)S(1)}, bf16[128,512]{1,0:T(8,128)(2,1)S(1)}, u32[]{:S(2)}, u32[]{:S(2)}) collective-permute-start(bf16[128,512]{1,0:T(8,128)(2,1)S(1)} %collective-permute-done.14.refs_4_), channel_id=1, source_target_pairs={{0,1},{1,0},{2,3},{3,2},{4,5},{5,4},{6,7},{7,6},{8,9},{9,8},{10,11... | collective-permute-start | bytes 393224 | tf_op jit(solution)/shard_map/ppermute | solution.py:27
  47.4 1.5 %collective-permute-start.17 = (bf16[128,512]{1,0:T(8,128)(2,1)S(1)}, bf16[128,512]{1,0:T(8,128)(2,1)S(1)}, u32[]{:S(2)}, u32[]{:S(2)}) collective-permute-start(bf16[128,512]{1,0:T(8,128)(2,1)S(1)} %collective-permute-done.16.refs_6_), channel_id=1, source_target_pairs={{0,1},{1,0},{2,3},{3,2},{4,5},{5,4},{6,7},{7,6},{8,9},{9,8},{10,11... | collective-permute-start | bytes 393224 | tf_op jit(solution)/shard_map/ppermute | solution.py:27
where the time goes:
time: 51.5 us; the launch traced here: 51.4 us
  waiting for transfers between devices  21.2 us (41%)
  starting transfers between devices  19.8 us (38%)
  Pallas kernels  9.58 us (19%)
  between operations  0.73 us (1%)
    ppermute x18, waiting for transfers between devices, swap(): return lax.ppermute(x, axis, [(i, i ^ mask) for i in range(size)])  21.2 us
    ppermute x18, starting transfers between devices, swap(): return lax.ppermute(x, axis, [(i, i ^ mask) for i in range(size)])  19.8 us
    pallas_call x1, Pallas kernels, project(): pl.pallas_call(project_kernel, out_shape=parts + parts, in_specs=[whole(p...  3.27 us
    pallas_call x1, Pallas kernels, back(): pl.pallas_call(functools.partial(back_kernel, owners), out_shape=jax.Shap...  2.41 us
    pallas_call x1, Pallas kernels, terms_of(): pl.pallas_call(term_kernel, out_shape=[jax.ShapeDtypeStruct((blk + (16 if...  1.31 us
    pallas_call x1, Pallas kernels, table_of(): pl.pallas_call(table_kernel, out_shape=(jax.ShapeDtypeStruct((DEEP, width...  1.05 us
  transfers between devices with their start and end apart: 18, of which 8 were waited for; matrix products, arithmetic and copies ran while one was open for 0% of the time, Pallas kernels for 7%

commit v1 on v0

--- a/solution.py
+++ b/solution.py
@@ -46,7 +46,7 @@
     targets, kernels, volume, acc, sems, target_sem = refs[7:]
     vblocks, top, blk, _ = kernels.shape
     near, half = send_near.shape[0], acc.shape[0] // 2
-    group = 4
+    group = 8
     steps = vblocks // group
 
     def copies(step):
@@ -65,7 +65,7 @@
     get_targets.wait()
     me = me_ref[0]
 
-    def body(step, carry):
+    for step in range(steps):
         for copy in copies(step):
             copy.wait()
         for i in range(group):
@@ -78,9 +78,6 @@
                 rel = targets[t, b] ^ me
                 slot = (rel & 1) * half + (rel >> 1)
                 acc[slot] += product[t * blk : (t + 1) * blk]
-        return carry
-
-    lax.fori_loop(0, steps, body, 0)
     send_far[...] = acc[half + near :].astype(BF16)
     send_near[...] = acc[half : half + near].astype(BF16)
     keep_far[...] = acc[near:half].astype(BF16)

time: 51.5 us -> 51.5 us (level)
  no operation moved by 1% of the time
where the time goes in v1:
time: 51.5 us; the launch traced here: 51.3 us
  waiting for transfers between devices  21.2 us (41%)
  starting transfers between devices  19.8 us (38%)
  Pallas kernels  9.51 us (18%)
  between operations  0.73 us (1%)
    ppermute x18, waiting for transfers between devices, swap(): return lax.ppermute(x, axis, [(i, i ^ mask) for i in range(size)])  21.2 us
    ppermute x18, starting transfers between devices, swap(): return lax.ppermute(x, axis, [(i, i ^ mask) for i in range(size)])  19.8 us
    pallas_call x1, Pallas kernels, project(): pl.pallas_call(project_kernel, out_shape=parts + parts, in_specs=[whole(p...  3.2 us
    pallas_call x1, Pallas kernels, back(): pl.pallas_call(functools.partial(back_kernel, owners), out_shape=jax.Shap...  2.42 us
    pallas_call x1, Pallas kernels, terms_of(): pl.pallas_call(term_kernel, out_shape=[jax.ShapeDtypeStruct((blk + (16 if...  1.3 us
    pallas_call x1, Pallas kernels, table_of(): pl.pallas_call(table_kernel, out_shape=(jax.ShapeDtypeStruct((DEEP, width...  1.04 us
  transfers between devices with their start and end apart: 18, of which 8 were waited for; matrix products, arithmetic and copies ran while one was open for 0% of the time, Pallas kernels for 7%

profile of v1, /device:TPU:0, one launch (start us, length us, event | category | flops | bytes accessed | tf_op | source)
XLA Modules:
  0.0 51.3 jit_solution(6154773853981746435)
XLA Ops:
  0.0 0.0 copy-start.2
  0.0 3.2 %project.1 = (bf16[2,128,512]{2,1,0:T(8,128)(2,1)S(1)}, bf16[2,128,512]{2,1,0:T(8,128)(2,1)S(1)}, bf16[2,128,512]{2,1,0:T(8,128)(2,1)S(1)}, bf16[2,128,512]{2,1,0:T(8,128)(2,1)S(1)}) custom-call(s32[1]{0:T(128)} %bitcast.me_ref, s32[2,16]{1,0:T(2,128)} %bitcast.4, bf16[16,2,128,128]{3,2,1,0:T(8,128)(2,1)} %kernels_ref.1, bf16[16,128,512]{2,1,0:T(8,128)(2,1)} %refs_2_.1), custom_call_target="tpu_custom_call" | custom-call | flops 536870912 | bytes 4194304 | tf_op jit(solution)/shard_map/project/pallas_call | solution.py:94
  3.2 0.6 %collective-permute-start = (bf16[2,128,512]{2,1,0:T(8,128)(2,1)S(1)}, bf16[2,128,512]{2,1,0:T(8,128)(2,1)S(1)}, u32[]{:S(2)}, u32[]{:S(2)}) collective-permute-start(bf16[2,128,512]{2,1,0:T(8,128)(2,1)S(1)} %get-tuple-element.24), channel_id=1, source_target_pairs={{0,1},{1,0},{2,3},{3,2},{4,5},{5,4},{6,7},{7,6},{8,9},{9,8},{10,11... | collective-permute-start | bytes 786440 | tf_op jit(solution)/shard_map/ppermute | solution.py:27
  3.8 0.1 collective-permute-start.2
  4.5 0.9 %circ.1 = (f32[8,128]{1,0:T(8,128)S(1)}, bf16[256,4096]{1,0:T(8,128)(2,1)S(1)}) custom-call(f32[1]{0:T(128)S(6)} %copy.6.number_ref), custom_call_target="tpu_custom_call" | custom-call | flops 16777216 | bytes 3145728 | tf_op jit(solution)/shard_map/circ/pallas_call | solution.py:209
  5.4 0.0 collective-permute-done.came_ref
  5.4 0.1 pair_sum.2
  5.5 3.1 %collective-permute-start.1 = (bf16[128,512]{1,0:T(8,128)(2,1)S(1)}, bf16[128,512]{1,0:T(8,128)(2,1)S(1)}, u32[]{:S(2)}, u32[]{:S(2)}) collective-permute-start(bf16[128,512]{1,0:T(8,128)(2,1)S(1)} %get-tuple-element.26), channel_id=1, source_target_pairs={{0,2},{1,3},{2,0},{3,1},{4,6},{5,7},{6,4},{7,5},{8,10},{9,11},{10,... | collective-permute-start | bytes 393224 | tf_op jit(solution)/shard_map/ppermute | solution.py:27
  8.6 0.0 copy-done.2
  8.6 1.3 %terms.1 = (bf16[128,512]{1,0:T(8,128)(2,1)S(1)}, bf16[144,512]{1,0:T(8,128)(2,1)S(1)}, bf16[144,512]{1,0:T(8,128)(2,1)S(1)}, bf16[144,512]{1,0:T(8,128)(2,1)S(1)}) custom-call(f32[8,128]{1,0:T(8,128)S(1)} %get-tuple-element.32.number_ref, s32[1]{0:T(128)} %bitcast.2.me_ref, bf16[128,2048]{1,0:T(8,128)(2,1)S(1)} %bitcast.6, ...), custom_call_target="tpu_custom_call" | custom-call | flops 1073741824 | bytes 3145728 | tf_op jit(solution)/shard_map/terms/pallas_call | solution.py:253
  9.9 1.6 %collective-permute-start.5 = (bf16[144,512]{1,0:T(8,128)(2,1)S(1)}, bf16[144,512]{1,0:T(8,128)(2,1)S(1)}, u32[]{:S(2)}, u32[]{:S(2)}) collective-permute-start(bf16[144,512]{1,0:T(8,128)(2,1)S(1)} %get-tuple-element.35), channel_id=1, source_target_pairs={{0,8},{8,0},{16,24},{24,16},{1,9},{9,1},{17,25},{25,17},{2,10},{10... | collective-permute-start | bytes 442376 | tf_op jit(solution)/shard_map/ppermute | solution.py:27
  11.4 0.0 collective-permute-done.2.came_ref
  11.4 0.0 copy-start
  11.4 0.0 copy-start.1
  11.4 0.1 pair_sum.3
  11.5 2.7 %collective-permute-start.3 = (bf16[128,512]{1,0:T(8,128)(2,1)S(1)}, bf16[128,512]{1,0:T(8,128)(2,1)S(1)}, u32[]{:S(2)}, u32[]{:S(2)}) collective-permute-start(bf16[128,512]{1,0:T(8,128)(2,1)S(1)} %get-tuple-element.29), channel_id=1, source_target_pairs={{0,4},{1,5},{2,6},{3,7},{4,0},{5,1},{6,2},{7,3},{8,12},{9,13},{10,... | collective-permute-start | bytes 393224 | tf_op jit(solution)/shard_map/ppermute | solution.py:27
  14.2 0.2 collective-permute-start.4
  14.4 1.5 %collective-permute-start.6 = (bf16[144,512]{1,0:T(8,128)(2,1)S(1)}, bf16[144,512]{1,0:T(8,128)(2,1)S(1)}, u32[]{:S(2)}, u32[]{:S(2)}) collective-permute-start(bf16[144,512]{1,0:T(8,128)(2,1)S(1)} %get-tuple-element.36), channel_id=1, source_target_pairs={{0,16},{8,24},{16,0},{24,8},{1,17},{9,25},{17,1},{25,9},{2,18},{10... | collective-permute-start | bytes 442376 | tf_op jit(solution)/shard_map/ppermute | solution.py:27
  15.9 0.0 collective-permute-done.1.refs_0_
  15.9 0.3 collective-permute-start.7
  16.2 6.8 %collective-permute-done.3.refs_1_ = bf16[128,512]{1,0:T(8,128)(2,1)S(1)} collective-permute-done((bf16[128,512]{1,0:T(8,128)(2,1)S(1)}, bf16[128,512]{1,0:T(8,128)(2,1)S(1)}, u32[]{:S(2)}, u32[]{:S(2)}) %collective-permute-start.3) | collective-permute-done | bytes 131104 | tf_op jit(solution)/shard_map/ppermute | solution.py:27
  23.0 0.0 collective-permute-done.4.refs_2_
  23.0 0.1 total_sum.1
  23.1 1.3 %collective-permute-start.8 = (bf16[128,512]{1,0:T(8,128)(2,1)S(1)}, bf16[128,512]{1,0:T(8,128)(2,1)S(1)}, u32[]{:S(2)}, u32[]{:S(2)}) collective-permute-start(bf16[128,512]{1,0:T(8,128)(2,1)S(1)} %get-tuple-element.40.refs_0_), channel_id=1, source_target_pairs={{0,8},{8,0},{16,24},{24,16},{1,9},{9,1},{17,25},{25,17},{2,10},{10... | collective-permute-start | bytes 393224 | tf_op jit(solution)/shard_map/ppermute | solution.py:27
  24.4 1.5 %collective-permute-start.9 = (bf16[128,512]{1,0:T(8,128)(2,1)S(1)}, bf16[128,512]{1,0:T(8,128)(2,1)S(1)}, u32[]{:S(2)}, u32[]{:S(2)}) collective-permute-start(bf16[128,512]{1,0:T(8,128)(2,1)S(1)} %get-tuple-element.40.refs_0_), channel_id=1, source_target_pairs={{0,16},{8,24},{16,0},{24,8},{1,17},{9,25},{17,1},{25,9},{2,18},{10... | collective-permute-start | bytes 393224 | tf_op jit(solution)/shard_map/ppermute | solution.py:27
  25.9 0.0 collective-permute-done.5.refs_1_
  25.9 0.7 %collective-permute-start.10 = (bf16[128,512]{1,0:T(8,128)(2,1)S(1)}, bf16[128,512]{1,0:T(8,128)(2,1)S(1)}, u32[]{:S(2)}, u32[]{:S(2)}) collective-permute-start(bf16[128,512]{1,0:T(8,128)(2,1)S(1)} %get-tuple-element.40.refs_0_), channel_id=1, source_target_pairs={{0,24},{8,16},{16,8},{24,0},{1,25},{9,17},{17,9},{25,1},{2,26},{10... | collective-permute-start | bytes 393224 | tf_op jit(solution)/shard_map/ppermute | solution.py:27
  26.6 0.0 collective-permute-done.6.refs_2_
  26.6 0.0 collective-permute-done.7.refs_3_
  26.6 1.0 %table.1 = (bf16[256,2560]{1,0:T(8,128)(2,1)S(1)}, f32[128,512]{1,0:T(8,128)S(1)}) custom-call(f32[8,128]{1,0:T(8,128)S(1)} %get-tuple-element.32.number_ref, bf16[128,512]{1,0:T(8,128)(2,1)S(1)} %get-tuple-element.34.refs_0_, bf16[144,512]{1,0:T(8,128)(2,1)S(1)} %collective-permute-done.5.refs_1_, bf16[144,512]{1,0:T(8,128)(2,1)S(1)} %collective-permute-done.6.refs_2_, ...), custom_call_target="tpu_custom_call" | custom-call | flops 16777216 | bytes 3145728 | tf_op jit(solution)/shard_map/table/pallas_call | solution.py:291
  27.7 1.8 %collective-permute-done.8.refs_1_ = bf16[128,512]{1,0:T(8,128)(2,1)S(1)} collective-permute-done((bf16[128,512]{1,0:T(8,128)(2,1)S(1)}, bf16[128,512]{1,0:T(8,128)(2,1)S(1)}, u32[]{:S(2)}, u32[]{:S(2)}) %collective-permute-start.8) | collective-permute-done | bytes 131104 | tf_op jit(solution)/shard_map/ppermute | solution.py:27
  29.5 1.4 %collective-permute-done.9.refs_2_ = bf16[128,512]{1,0:T(8,128)(2,1)S(1)} collective-permute-done((bf16[128,512]{1,0:T(8,128)(2,1)S(1)}, bf16[128,512]{1,0:T(8,128)(2,1)S(1)}, u32[]{:S(2)}, u32[]{:S(2)}) %collective-permute-start.9) | collective-permute-done | bytes 131104 | tf_op jit(solution)/shard_map/ppermute | solution.py:27
  30.9 1.3 %collective-permute-done.10.refs_3_ = bf16[128,512]{1,0:T(8,128)(2,1)S(1)} collective-permute-done((bf16[128,512]{1,0:T(8,128)(2,1)S(1)}, bf16[128,512]{1,0:T(8,128)(2,1)S(1)}, u32[]{:S(2)}, u32[]{:S(2)}) %collective-permute-start.10) | collective-permute-done | bytes 131104 | tf_op jit(solution)/shard_map/ppermute | solution.py:27
  32.2 0.4 filter.1.refs_0_
  32.7 3.4 %collective-permute-start.12 = (bf16[128,512]{1,0:T(8,128)(2,1)S(1)}, bf16[128,512]{1,0:T(8,128)(2,1)S(1)}, u32[]{:S(2)}, u32[]{:S(2)}) collective-permute-start(bf16[128,512]{1,0:T(8,128)(2,1)S(1)} %filter.1.refs_0_), channel_id=1, source_target_pairs={{0,2},{1,3},{2,0},{3,1},{4,6},{5,7},{6,4},{7,5},{8,10},{9,11},{10,... | collective-permute-start | bytes 393224 | tf_op jit(solution)/shard_map/ppermute | solution.py:27
  36.1 0.2 collective-permute-start.14
  36.3 2.2 %collective-permute-start.16 = (bf16[128,512]{1,0:T(8,128)(2,1)S(1)}, bf16[128,512]{1,0:T(8,128)(2,1)S(1)}, u32[]{:S(2)}, u32[]{:S(2)}) collective-permute-start(bf16[128,512]{1,0:T(8,128)(2,1)S(1)} %filter.1.refs_0_), channel_id=1, source_target_pairs={{0,6},{1,7},{2,4},{3,5},{4,2},{5,3},{6,0},{7,1},{8,14},{9,15},{10,... | collective-permute-start | bytes 393224 | tf_op jit(solution)/shard_map/ppermute | solution.py:27
  38.6 0.0 collective-permute-start.11
  38.6 1.4 %collective-permute-done.12.refs_2_ = bf16[128,512]{1,0:T(8,128)(2,1)S(1)} collective-permute-done((bf16[128,512]{1,0:T(8,128)(2,1)S(1)}, bf16[128,512]{1,0:T(8,128)(2,1)S(1)}, u32[]{:S(2)}, u32[]{:S(2)}) %collective-permute-start.12) | collective-permute-done | bytes 131104 | tf_op jit(solution)/shard_map/ppermute | solution.py:27
  40.0 0.0 collective-permute-start.13
  40.0 7.4 %collective-permute-done.14.refs_4_ = bf16[128,512]{1,0:T(8,128)(2,1)S(1)} collective-permute-done((bf16[128,512]{1,0:T(8,128)(2,1)S(1)}, bf16[128,512]{1,0:T(8,128)(2,1)S(1)}, u32[]{:S(2)}, u32[]{:S(2)}) %collective-permute-start.14) | collective-permute-done | bytes 131104 | tf_op jit(solution)/shard_map/ppermute | solution.py:27
  47.4 0.0 collective-permute-start.15
  47.4 0.0 collective-permute-done.16.refs_6_
  47.4 0.5 collective-permute-start.17
  47.9 0.0 collective-permute-done.11.refs_1_
  47.9 0.0 collective-permute-done.13.refs_3_
  47.9 0.8 %collective-permute-done.15.refs_5_ = bf16[128,512]{1,0:T(8,128)(2,1)S(1)} collective-permute-done((bf16[128,512]{1,0:T(8,128)(2,1)S(1)}, bf16[128,512]{1,0:T(8,128)(2,1)S(1)}, u32[]{:S(2)}, u32[]{:S(2)}) %collective-permute-start.15) | collective-permute-done | bytes 131104 | tf_op jit(solution)/shard_map/ppermute | solution.py:27
  48.7 0.2 collective-permute-done.17.refs_7_
  48.9 0.0 copy-done
  48.9 0.0 copy-done.1
  48.9 2.4 %back.1 = bf16[16,128,512]{2,1,0:T(8,128)(2,1)} custom-call(s32[1]{0:T(128)} %bitcast.me_ref, s32[2,16]{1,0:T(2,128)S(1)} %bitcast.5, bf16[16,2,128,128]{3,2,1,0:T(8,128)(2,1)S(1)} %copy-done, bf16[128,512]{1,0:T(8,128)(2,1)S(1)} %filter.1.refs_0_, bf16[128,512]{1,0:T(8,128)(2,1)S(1)} %collective-permute-done.11.refs_1_, ...), custom_call_target="tpu_custom_call" | custom-call | flops 536870912 | bytes 4194304 | tf_op jit(solution)/shard_map/back/pallas_call | solution.py:368
Async XLA Ops:
  0.0 8.6 %copy-start.2 = (bf16[1,1,128,2048]{3,2,1,0:T(8,128)(2,1)S(1)}, bf16[1,1,128,2048]{3,2,1,0:T(8,128)(2,1)}, u32[]{:S(2)}) copy-start(bf16[1,1,128,2048]{3,2,1,0:T(8,128)(2,1)} %param.8) | copy-start | bytes 1572868
  3.2 2.2 %collective-permute-start = (bf16[2,128,512]{2,1,0:T(8,128)(2,1)S(1)}, bf16[2,128,512]{2,1,0:T(8,128)(2,1)S(1)}, u32[]{:S(2)}, u32[]{:S(2)}) collective-permute-start(bf16[2,128,512]{2,1,0:T(8,128)(2,1)S(1)} %get-tuple-element.24), channel_id=1, source_target_pairs={{0,1},{1,0},{2,3},{3,2},{4,5},{5,4},{6,7},{7,6},{8,9},{9,8},{10,11... | collective-permute-start | bytes 786440 | tf_op jit(solution)/shard_map/ppermute | solution.py:27
  3.8 7.7 %collective-permute-start.2 = (bf16[2,128,512]{2,1,0:T(8,128)(2,1)S(1)}, bf16[2,128,512]{2,1,0:T(8,128)(2,1)S(1)}, u32[]{:S(2)}, u32[]{:S(2)}) collective-permute-start(bf16[2,128,512]{2,1,0:T(8,128)(2,1)S(1)} %get-tuple-element.28), channel_id=1, source_target_pairs={{0,1},{1,0},{2,3},{3,2},{4,5},{5,4},{6,7},{7,6},{8,9},{9,8},{10,11... | collective-permute-start | bytes 786440 | tf_op jit(solution)/shard_map/ppermute | solution.py:27
  5.5 10.4 %collective-permute-start.1 = (bf16[128,512]{1,0:T(8,128)(2,1)S(1)}, bf16[128,512]{1,0:T(8,128)(2,1)S(1)}, u32[]{:S(2)}, u32[]{:S(2)}) collective-permute-start(bf16[128,512]{1,0:T(8,128)(2,1)S(1)} %get-tuple-element.26), channel_id=1, source_target_pairs={{0,2},{1,3},{2,0},{3,1},{4,6},{5,7},{6,4},{7,5},{8,10},{9,11},{10,... | collective-permute-start | bytes 393224 | tf_op jit(solution)/shard_map/ppermute | solution.py:27
  9.9 16.0 %collective-permute-start.5 = (bf16[144,512]{1,0:T(8,128)(2,1)S(1)}, bf16[144,512]{1,0:T(8,128)(2,1)S(1)}, u32[]{:S(2)}, u32[]{:S(2)}) collective-permute-start(bf16[144,512]{1,0:T(8,128)(2,1)S(1)} %get-tuple-element.35), channel_id=1, source_target_pairs={{0,8},{8,0},{16,24},{24,16},{1,9},{9,1},{17,25},{25,17},{2,10},{10... | collective-permute-start | bytes 442376 | tf_op jit(solution)/shard_map/ppermute | solution.py:27
  11.4 37.5 %copy-start = (bf16[16,2,128,128]{3,2,1,0:T(8,128)(2,1)S(1)}, bf16[16,2,128,128]{3,2,1,0:T(8,128)(2,1)}, u32[]{:S(2)}) copy-start(bf16[16,2,128,128]{3,2,1,0:T(8,128)(2,1)} %kernels_ref.1) | copy-start | bytes 3145732
  11.4 37.5 %copy-start.1 = (s32[16,2]{0,1:T(2,128)S(1)}, s32[16,2]{0,1:T(2,128)}, u32[]{:S(2)}) copy-start(s32[16,2]{0,1:T(2,128)} %param.7) | copy-start | bytes 388
  11.5 11.5 %collective-permute-start.3 = (bf16[128,512]{1,0:T(8,128)(2,1)S(1)}, bf16[128,512]{1,0:T(8,128)(2,1)S(1)}, u32[]{:S(2)}, u32[]{:S(2)}) collective-permute-start(bf16[128,512]{1,0:T(8,128)(2,1)S(1)} %get-tuple-element.29), channel_id=1, source_target_pairs={{0,4},{1,5},{2,6},{3,7},{4,0},{5,1},{6,2},{7,3},{8,12},{9,13},{10,... | collective-permute-start | bytes 393224 | tf_op jit(solution)/shard_map/ppermute | solution.py:27
  14.2 8.8 %collective-permute-start.4 = (bf16[128,512]{1,0:T(8,128)(2,1)S(1)}, bf16[128,512]{1,0:T(8,128)(2,1)S(1)}, u32[]{:S(2)}, u32[]{:S(2)}) collective-permute-start(bf16[128,512]{1,0:T(8,128)(2,1)S(1)} %get-tuple-element.30), channel_id=1, source_target_pairs={{0,6},{1,7},{2,4},{3,5},{4,2},{5,3},{6,0},{7,1},{8,14},{9,15},{10,... | collective-permute-start | bytes 393224 | tf_op jit(solution)/shard_map/ppermute | solution.py:27
  14.4 12.3 %collective-permute-start.6 = (bf16[144,512]{1,0:T(8,128)(2,1)S(1)}, bf16[144,512]{1,0:T(8,128)(2,1)S(1)}, u32[]{:S(2)}, u32[]{:S(2)}) collective-permute-start(bf16[144,512]{1,0:T(8,128)(2,1)S(1)} %get-tuple-element.36), channel_id=1, source_target_pairs={{0,16},{8,24},{16,0},{24,8},{1,17},{9,25},{17,1},{25,9},{2,18},{10... | collective-permute-start | bytes 442376 | tf_op jit(solution)/shard_map/ppermute | solution.py:27
  15.9 10.7 %collective-permute-start.7 = (bf16[144,512]{1,0:T(8,128)(2,1)S(1)}, bf16[144,512]{1,0:T(8,128)(2,1)S(1)}, u32[]{:S(2)}, u32[]{:S(2)}) collective-permute-start(bf16[144,512]{1,0:T(8,128)(2,1)S(1)} %get-tuple-element.37), channel_id=1, source_target_pairs={{0,24},{8,16},{16,8},{24,0},{1,25},{9,17},{17,9},{25,1},{2,26},{10... | collective-permute-start | bytes 442376 | tf_op jit(solution)/shard_map/ppermute | solution.py:27
  23.1 6.4 %collective-permute-start.8 = (bf16[128,512]{1,0:T(8,128)(2,1)S(1)}, bf16[128,512]{1,0:T(8,128)(2,1)S(1)}, u32[]{:S(2)}, u32[]{:S(2)}) collective-permute-start(bf16[128,512]{1,0:T(8,128)(2,1)S(1)} %get-tuple-element.40.refs_0_), channel_id=1, source_target_pairs={{0,8},{8,0},{16,24},{24,16},{1,9},{9,1},{17,25},{25,17},{2,10},{10... | collective-permute-start | bytes 393224 | tf_op jit(solution)/shard_map/ppermute | solution.py:27
  24.4 6.5 %collective-permute-start.9 = (bf16[128,512]{1,0:T(8,128)(2,1)S(1)}, bf16[128,512]{1,0:T(8,128)(2,1)S(1)}, u32[]{:S(2)}, u32[]{:S(2)}) collective-permute-start(bf16[128,512]{1,0:T(8,128)(2,1)S(1)} %get-tuple-element.40.refs_0_), channel_id=1, source_target_pairs={{0,16},{8,24},{16,0},{24,8},{1,17},{9,25},{17,1},{25,9},{2,18},{10... | collective-permute-start | bytes 393224 | tf_op jit(solution)/shard_map/ppermute | solution.py:27
  25.9 6.3 %collective-permute-start.10 = (bf16[128,512]{1,0:T(8,128)(2,1)S(1)}, bf16[128,512]{1,0:T(8,128)(2,1)S(1)}, u32[]{:S(2)}, u32[]{:S(2)}) collective-permute-start(bf16[128,512]{1,0:T(8,128)(2,1)S(1)} %get-tuple-element.40.refs_0_), channel_id=1, source_target_pairs={{0,24},{8,16},{16,8},{24,0},{1,25},{9,17},{17,9},{25,1},{2,26},{10... | collective-permute-start | bytes 393224 | tf_op jit(solution)/shard_map/ppermute | solution.py:27
  32.7 7.3 %collective-permute-start.12 = (bf16[128,512]{1,0:T(8,128)(2,1)S(1)}, bf16[128,512]{1,0:T(8,128)(2,1)S(1)}, u32[]{:S(2)}, u32[]{:S(2)}) collective-permute-start(bf16[128,512]{1,0:T(8,128)(2,1)S(1)} %filter.1.refs_0_), channel_id=1, source_target_pairs={{0,2},{1,3},{2,0},{3,1},{4,6},{5,7},{6,4},{7,5},{8,10},{9,11},{10,... | collective-permute-start | bytes 393224 | tf_op jit(solution)/shard_map/ppermute | solution.py:27
  36.1 11.3 %collective-permute-start.14 = (bf16[128,512]{1,0:T(8,128)(2,1)S(1)}, bf16[128,512]{1,0:T(8,128)(2,1)S(1)}, u32[]{:S(2)}, u32[]{:S(2)}) collective-permute-start(bf16[128,512]{1,0:T(8,128)(2,1)S(1)} %filter.1.refs_0_), channel_id=1, source_target_pairs={{0,4},{1,5},{2,6},{3,7},{4,0},{5,1},{6,2},{7,3},{8,12},{9,13},{10,... | collective-permute-start | bytes 393224 | tf_op jit(solution)/shard_map/ppermute | solution.py:27
  36.3 11.1 %collective-permute-start.16 = (bf16[128,512]{1,0:T(8,128)(2,1)S(1)}, bf16[128,512]{1,0:T(8,128)(2,1)S(1)}, u32[]{:S(2)}, u32[]{:S(2)}) collective-permute-start(bf16[128,512]{1,0:T(8,128)(2,1)S(1)} %filter.1.refs_0_), channel_id=1, source_target_pairs={{0,6},{1,7},{2,4},{3,5},{4,2},{5,3},{6,0},{7,1},{8,14},{9,15},{10,... | collective-permute-start | bytes 393224 | tf_op jit(solution)/shard_map/ppermute | solution.py:27
  38.6 9.3 %collective-permute-start.11 = (bf16[128,512]{1,0:T(8,128)(2,1)S(1)}, bf16[128,512]{1,0:T(8,128)(2,1)S(1)}, u32[]{:S(2)}, u32[]{:S(2)}) collective-permute-start(bf16[128,512]{1,0:T(8,128)(2,1)S(1)} %filter.1.refs_0_), channel_id=1, source_target_pairs={{0,1},{1,0},{2,3},{3,2},{4,5},{5,4},{6,7},{7,6},{8,9},{9,8},{10,11... | collective-permute-start | bytes 393224 | tf_op jit(solution)/shard_map/ppermute | solution.py:27
  40.0 7.9 %collective-permute-start.13 = (bf16[128,512]{1,0:T(8,128)(2,1)S(1)}, bf16[128,512]{1,0:T(8,128)(2,1)S(1)}, u32[]{:S(2)}, u32[]{:S(2)}) collective-permute-start(bf16[128,512]{1,0:T(8,128)(2,1)S(1)} %collective-permute-done.12.refs_2_), channel_id=1, source_target_pairs={{0,1},{1,0},{2,3},{3,2},{4,5},{5,4},{6,7},{7,6},{8,9},{9,8},{10,11... | collective-permute-start | bytes 393224 | tf_op jit(solution)/shard_map/ppermute | solution.py:27
  47.4 1.3 %collective-permute-start.15 = (bf16[128,512]{1,0:T(8,128)(2,1)S(1)}, bf16[128,512]{1,0:T(8,128)(2,1)S(1)}, u32[]{:S(2)}, u32[]{:S(2)}) collective-permute-start(bf16[128,512]{1,0:T(8,128)(2,1)S(1)} %collective-permute-done.14.refs_4_), channel_id=1, source_target_pairs={{0,1},{1,0},{2,3},{3,2},{4,5},{5,4},{6,7},{7,6},{8,9},{9,8},{10,11... | collective-permute-start | bytes 393224 | tf_op jit(solution)/shard_map/ppermute | solution.py:27
  47.4 1.5 %collective-permute-start.17 = (bf16[128,512]{1,0:T(8,128)(2,1)S(1)}, bf16[128,512]{1,0:T(8,128)(2,1)S(1)}, u32[]{:S(2)}, u32[]{:S(2)}) collective-permute-start(bf16[128,512]{1,0:T(8,128)(2,1)S(1)} %collective-permute-done.16.refs_6_), channel_id=1, source_target_pairs={{0,1},{1,0},{2,3},{3,2},{4,5},{5,4},{6,7},{7,6},{8,9},{9,8},{10,11... | collective-permute-start | bytes 393224 | tf_op jit(solution)/shard_map/ppermute | solution.py:27
